TPU v7x, 32 devices: a whole 2x2x4 slice. The times are simulated.
32 devices in a mesh: rows: 16 (over z, y, x), cols: 2 (over core).
Axes of the slice: x: 2, y: 2, z: 4, core: 2. Of those that a mesh axis runs over, the one named last changes fastest.
Arguments:
- rhs: float32 [8192, 4096], P('rows', 'cols'), may hold values from -6 to 6
- leaf_v: float32 [8192, 256], P(('rows', 'cols')), may hold values from -8 to 8, as said below
- leaf_t: float32 [4096, 256], P('rows'), may hold values from -4 to 4, as said below
- merge_v: float32 [4, 4096, 256], P(None, 'rows'), may hold values from -4 to 4, as said below
- merge_t: float32 [4, 4096, 256], P(None, 'rows'), may hold values from -4 to 4, as said below
Outputs:
- applied: float32 [8192, 4096], P('rows', 'cols')
Inputs may be any that keep to these rules, and one draw needn't show every extreme that they name: leaf_v block d is zero above its diagonal and one on it. leaf_t blocks are upper triangular. At level j, merge_v block d is the identity where bit log2(16) - 1 - j of d is 0, and upper triangular where it is 1. merge_t blocks are upper triangular, and at level j the blocks of devices d and d xor 2**(log2(16) - 1 - j) are equal.
All inputs are finite; a program needn't handle non-finite values.
Results may differ from a plain program's by a relative error of at most 0.0001.
Values sent between devices are 32-bit elements; how exact they have to be, the bound alone decides.
A program may use at most 64 MiB of HBM per device.

v0:
```python
import jax
import jax.numpy as jnp
from jax import lax
from jax.sharding import PartitionSpec as P

HIGH = lax.Precision.HIGHEST


def from_partner(value, axis, apart):
    return lax.ppermute(value, axis, [(i, i ^ 1 << apart) for i in range(lax.axis_size(axis))])


def body(rhs, leaf_v, leaf_t, merge_v, merge_t):
    panel_width = leaf_t.shape[1]
    whole_refl = lax.all_gather(leaf_v, "cols", axis=0, tiled=True)
    upper_rows = rhs[:panel_width]
    lower_rows = rhs[panel_width:]
    tree_depth = lax.axis_size("rows").bit_length() - 1
    for level_index in range(merge_v.shape[0]):
        distance_bit = tree_depth - 1 - level_index
        merge_block = merge_v[level_index]
        merge_tri = merge_t[level_index]
        own_terms = jnp.einsum("nk,nj->kj", merge_block, upper_rows, precision=HIGH)
        partner = from_partner(own_terms, "rows", distance_bit)
        weights = jnp.dot(merge_tri, own_terms + partner, precision=HIGH)
        upper_rows = upper_rows - jnp.dot(merge_block, weights, precision=HIGH)
    stacked = jnp.concatenate([upper_rows, lower_rows], axis=0)
    leaf_proj = jnp.einsum("nk,nj->kj", whole_refl, stacked, precision=HIGH)
    inner = jnp.dot(leaf_t, leaf_proj, precision=HIGH)
    return stacked - jnp.dot(whole_refl, inner, precision=HIGH)


def solution(mesh):
    return jax.shard_map(
        body,
        mesh=mesh,
        in_specs=(
            P("rows", "cols"),
            P(("rows", "cols"), None),
            P("rows", None),
            P(None, "rows", None),
            P(None, "rows", None),
        ),
        out_specs=P("rows", "cols"),
        check_vma=False,
    )
```

profile of v0, /device:TPU:0, one launch (start us, length us, event | category | flops | bytes accessed | tf_op | source)
XLA Modules:
  0.0 291.1 jit_solution(15127945032142349599)
XLA Ops:
  0.0 0.0 copy-start
  0.0 0.0 copy-start.3
  0.0 3.7 %fusion.13 = f32[256,2048]{1,0:T(8,128)S(1)} fusion(f32[512,2048]{1,0:T(8,128)} %param.5, f32[4,256,256]{2,1,0:T(8,128)} %param.8), kind=kOutput, calls=%fused_computation.22 | convolution fusion | flops 1610612736 | bytes 4456448 | tf_op jit(solution)/shard_map/nk,nj->kj/dot_general | solution.py:23
  3.7 0.0 copy-start.1
  3.7 0.0 copy-start.2
  3.7 4.1 %collective-permute-start = (f32[256,2048]{1,0:T(8,128)S(1)}, f32[256,2048]{1,0:T(8,128)S(1)}, u32[]{:S(2)}, u32[]{:S(2)}) collective-permute-start(f32[256,2048]{1,0:T(8,128)S(1)} %fusion.13), channel_id=1, source_target_pairs={{0,16},{2,18},{4,20},{6,22},{8,24},{10,26},{12,28},{14,30},{16,0},... | collective-permute-start | bytes 6291464 | tf_op jit(solution)/shard_map/ppermute | solution.py:10
  7.8 90.6 %collective-permute-done = f32[256,2048]{1,0:T(8,128)S(1)} collective-permute-done((f32[256,2048]{1,0:T(8,128)S(1)}, f32[256,2048]{1,0:T(8,128)S(1)}, u32[]{:S(2)}, u32[]{:S(2)}) %collective-permute-start) | collective-permute-done | bytes 2097184 | tf_op jit(solution)/shard_map/ppermute | solution.py:10
  98.4 0.0 copy-done.3
  98.4 3.6 %fusion.11 = f32[2048,256]{1,0:T(8,128)S(1)} fusion(f32[256,2048]{1,0:T(8,128)S(1)} %fusion.13, f32[256,2048]{1,0:T(8,128)S(1)} %collective-permute-done, f32[4,256,256]{2,1,0:T(8,128)S(1)} %copy-done.3), kind=kOutput, calls=%fused_computation.20 | convolution fusion | flops 1611137024 | bytes 6553600 | tf_op jit(solution)/shard_map/dot_general | solution.py:25
  102.0 0.0 copy-done.1
  102.0 0.0 copy-done.2
  102.0 2.1 fusion.4
  104.1 3.6 %convolution_bitcast_fusion.5 = f32[256,2048]{0,1:T(8,128)S(1)} fusion(f32[256,2048]{1,0:T(8,128)S(1)} %fusion.4, f32[4,256,256]{2,1,0:T(8,128)S(1)} %copy-done.2), kind=kOutput, calls=%fused_computation.11 | convolution fusion | flops 1610612736 | bytes 4456448 | tf_op jit(solution)/shard_map/nk,nj->kj/dot_general | solution.py:23
  107.7 0.8 collective-permute-start.1
  108.5 46.1 %collective-permute-done.1 = f32[256,2048]{0,1:T(8,128)S(1)} collective-permute-done((f32[256,2048]{0,1:T(8,128)S(1)}, f32[256,2048]{0,1:T(8,128)S(1)}, u32[]{:S(2)}, u32[]{:S(2)}) %collective-permute-start.1) | collective-permute-done | bytes 2097184 | tf_op jit(solution)/shard_map/ppermute | solution.py:10
  154.5 2.2 fusion.9
  156.7 2.1 fusion.3
  158.8 3.6 %convolution_bitcast_fusion.3 = f32[256,2048]{0,1:T(8,128)S(1)} fusion(f32[256,2048]{1,0:T(8,128)S(1)} %fusion.3, f32[4,256,256]{2,1,0:T(8,128)S(1)} %copy-done.2), kind=kOutput, calls=%fused_computation.8 | convolution fusion | flops 1610612736 | bytes 4456448 | tf_op jit(solution)/shard_map/nk,nj->kj/dot_general | solution.py:23
  162.4 1.3 collective-permute-start.2
  163.7 44.6 %collective-permute-done.2 = f32[256,2048]{0,1:T(8,128)S(1)} collective-permute-done((f32[256,2048]{0,1:T(8,128)S(1)}, f32[256,2048]{0,1:T(8,128)S(1)}, u32[]{:S(2)}, u32[]{:S(2)}) %collective-permute-start.2) | collective-permute-done | bytes 2097184 | tf_op jit(solution)/shard_map/ppermute | solution.py:10
  208.3 1.9 fusion.7
  210.3 2.1 fusion.2
  212.3 15.1 %convolution_bitcast_fusion.1 = f32[256,2048]{0,1:T(8,128)S(1)} fusion(f32[256,2048]{1,0:T(8,128)S(1)} %fusion.2, f32[4,256,256]{2,1,0:T(8,128)S(1)} %copy-done.2), kind=kOutput, calls=%fused_computation.5 | convolution fusion | flops 1610612736 | bytes 4456448 | tf_op jit(solution)/shard_map/nk,nj->kj/dot_general | solution.py:23
  227.5 0.0 copy-start.4
  227.5 1.3 collective-permute-start.3
  228.8 0.1 slice.39
  229.0 0.0 copy-done.4
  229.0 2.2 all_gather.3
  231.1 41.4 %collective-permute-done.3 = f32[256,2048]{0,1:T(8,128)S(1)} collective-permute-done((f32[256,2048]{0,1:T(8,128)S(1)}, f32[256,2048]{0,1:T(8,128)S(1)}, u32[]{:S(2)}, u32[]{:S(2)}) %collective-permute-start.3) | collective-permute-done | bytes 2097184 | tf_op jit(solution)/shard_map/ppermute | solution.py:10
  272.5 1.9 fusion.5
  274.4 2.1 fusion.1
  276.5 7.1 %fusion = f32[2048,256]{1,0:T(8,128)S(1)} fusion(f32[512,256]{1,0:T(8,128)S(1)} %all_gather.3, f32[256,2048]{1,0:T(8,128)S(1)} %slice.39, f32[256,2048]{1,0:T(8,128)S(1)} %fusion.1), kind=kOutput, calls=%fused_computation.2 | convolution fusion | flops 3222274048 | bytes 6815744 | tf_op jit(solution)/shard_map/nk,nj->kj/dot_general | solution.py:28
  283.6 0.0 copy-done
  283.6 1.9 fusion.40
  285.6 5.3 %bitcast_subtract_fusion = f32[512,2048]{1,0:T(8,128)} fusion(f32[256,2048]{1,0:T(8,128)S(1)} %slice.39, f32[256,2048]{1,0:T(8,128)S(1)} %fusion.1, f32[2048,256]{1,0:T(8,128)S(1)} %fusion.40, f32[512,256]{1,0:T(8,128)S(1)} %all_gather.3), kind=kOutput, calls=%fused_computation.1 | convolution fusion | flops 3223322624 | bytes 11010048 | tf_op jit(solution)/shard_map/dot_general | solution.py:30
Async XLA Ops:
  0.0 283.6 %copy-start = (f32[256,256]{1,0:T(8,128)S(1)}, f32[256,256]{1,0:T(8,128)}, u32[]{:S(2)}) copy-start(f32[256,256]{1,0:T(8,128)} %param.7) | copy-start | bytes 786436
  0.0 98.4 %copy-start.3 = (f32[4,256,256]{2,1,0:T(8,128)S(1)}, f32[4,256,256]{2,1,0:T(8,128)}, u32[]{:S(2)}) copy-start(f32[4,256,256]{2,1,0:T(8,128)} %param.9) | copy-start | bytes 3145732
  3.7 98.3 %copy-start.1 = (f32[512,2048]{1,0:T(8,128)S(1)}, f32[512,2048]{1,0:T(8,128)}, u32[]{:S(2)}) copy-start(f32[512,2048]{1,0:T(8,128)} %param.5) | copy-start | bytes 12582916
  3.7 98.3 %copy-start.2 = (f32[4,256,256]{2,1,0:T(8,128)S(1)}, f32[4,256,256]{2,1,0:T(8,128)}, u32[]{:S(2)}) copy-start(f32[4,256,256]{2,1,0:T(8,128)} %param.8) | copy-start | bytes 3145732
  3.7 94.7 %collective-permute-start = (f32[256,2048]{1,0:T(8,128)S(1)}, f32[256,2048]{1,0:T(8,128)S(1)}, u32[]{:S(2)}, u32[]{:S(2)}) collective-permute-start(f32[256,2048]{1,0:T(8,128)S(1)} %fusion.13), channel_id=1, source_target_pairs={{0,16},{2,18},{4,20},{6,22},{8,24},{10,26},{12,28},{14,30},{16,0},... | collective-permute-start | bytes 6291464 | tf_op jit(solution)/shard_map/ppermute | solution.py:10
  107.7 46.9 %collective-permute-start.1 = (f32[256,2048]{0,1:T(8,128)S(1)}, f32[256,2048]{0,1:T(8,128)S(1)}, u32[]{:S(2)}, u32[]{:S(2)}) collective-permute-start(f32[256,2048]{0,1:T(8,128)S(1)} %convolution_bitcast_fusion.5), channel_id=1, source_target_pairs={{0,8},{2,10},{4,12},{6,14},{8,0},{10,2},{12,4},{14,6},{16,24},{18,... | collective-permute-start | bytes 6291464 | tf_op jit(solution)/shard_map/ppermute | solution.py:10
  162.4 46.0 %collective-permute-start.2 = (f32[256,2048]{0,1:T(8,128)S(1)}, f32[256,2048]{0,1:T(8,128)S(1)}, u32[]{:S(2)}, u32[]{:S(2)}) collective-permute-start(f32[256,2048]{0,1:T(8,128)S(1)} %convolution_bitcast_fusion.3), channel_id=1, source_target_pairs={{0,4},{2,6},{4,0},{6,2},{8,12},{10,14},{12,8},{14,10},{16,20},{18,... | collective-permute-start | bytes 6291464 | tf_op jit(solution)/shard_map/ppermute | solution.py:10
  227.5 1.5 copy-start.4
  227.5 45.0 %collective-permute-start.3 = (f32[256,2048]{0,1:T(8,128)S(1)}, f32[256,2048]{0,1:T(8,128)S(1)}, u32[]{:S(2)}, u32[]{:S(2)}) collective-permute-start(f32[256,2048]{0,1:T(8,128)S(1)} %convolution_bitcast_fusion.1), channel_id=1, source_target_pairs={{0,2},{2,0},{4,6},{6,4},{8,10},{10,8},{12,14},{14,12},{16,18},{18,... | collective-permute-start | bytes 6291464 | tf_op jit(solution)/shard_map/ppermute | solution.py:10
where the time goes:
time: 295 us; the launch traced here: 291 us
  waiting for transfers between devices  223 us (76%)
  matrix products  58.1 us (20%)
  starting transfers between devices  7.55 us (3%)
    ppermute x4, waiting for transfers between devices, from_partner(): lax.ppermute(value, axis, [(i, i ^ 1 << apart) for i in range(lax.axis_si...  223 us
    dot_general x4, matrix products, body(): own_terms = jnp.einsum('nk,nj->kj', merge_block, upper_rows, precision=HIGH)  25.9 us
    dot_general x4, matrix products, body(): weights = jnp.dot(merge_tri, own_terms + partner, precision=HIGH)  9.61 us
    dot_general x4, matrix products, body(): upper_rows = upper_rows - jnp.dot(merge_block, weights, precision=HIGH)  8.3 us
    ppermute x4, starting transfers between devices, from_partner(): lax.ppermute(value, axis, [(i, i ^ 1 << apart) for i in range(lax.axis_si...  7.55 us
    dot_general x1, matrix products, body(): leaf_proj = jnp.einsum('nk,nj->kj', whole_refl, stacked, precision=HIGH)  7.07 us
  transfers between devices with their start and end apart: 4, of which 4 were waited for; matrix products, arithmetic and copies ran while one was open for 0% of the time, Pallas kernels for 0%

commit v1 on v0

v1 whole, which is shorter than its diff:
```python
import functools

import jax
import jax.numpy as jnp
from jax import lax
from jax.experimental import pallas as pl
from jax.experimental.pallas import tpu as pltpu
from jax.sharding import PartitionSpec as P

MESH = pl.DeviceIdType.MESH
WIDTH = 128
LOOK = 3
FIRST_LAG = 2


def split_rows(w):
    hi = w.astype(jnp.bfloat16)
    lo = (w - hi.astype(jnp.float32)).astype(jnp.bfloat16)
    return jnp.concatenate([hi, lo], axis=0)


def split_cols(x):
    hi = x.astype(jnp.bfloat16)
    lo = (x - hi.astype(jnp.float32)).astype(jnp.bfloat16)
    return jnp.concatenate([hi, lo], axis=1)


def times(w_ref, x):
    m, n = w_ref.shape[0] // 2, x.shape[1]
    p = jnp.dot(w_ref[...], split_cols(x), preferred_element_type=jnp.float32)
    return (p[:m, :n] + p[:m, n:]) + (p[m:, :n] + p[m:, n:])


def kernel(
    rhs, leaf_v, leaf_t, merge_v, merge_t, out,
    x, sent, got, mv, mt, lv, lt, v2, vt2, t2, l2, lt2, r2,
    up_sem, low_sem, out_sem, mv_sem, mt_sem, lv_sem, lt_sem, leaf_send, leaf_recv, send_sem, recv_sem,
):
    levels, width = merge_v.shape[0], leaf_t.shape[1]
    chunks = x.shape[0]
    depth = lax.axis_size("rows").bit_length() - 1
    row, col = lax.axis_index("rows"), lax.axis_index("cols")
    partners = []
    for j in range(levels):
        stride = 1 << (depth - 1 - j)
        partners.append(row + stride * (1 - 2 * ((row // stride) % 2)))

    def columns(c):
        return pl.ds(pl.multiple_of(c * WIDTH, WIDTH), WIDTH)

    def upper_copy(c):
        return pltpu.make_async_copy(rhs.at[pl.ds(0, width), columns(c)], x.at[c, pl.ds(0, width)], up_sem.at[c])

    def lower_copy(c):
        low = pl.ds(width, x.shape[1] - width)
        return pltpu.make_async_copy(rhs.at[low, columns(c)], x.at[c, low], low_sem.at[c])

    def out_copy(c):
        return pltpu.make_async_copy(x.at[c], out.at[:, columns(c)], out_sem.at[c])

    def exchange(j, c):
        return pltpu.make_async_remote_copy(
            src_ref=sent.at[j, c], dst_ref=got.at[j, c],
            send_sem=send_sem.at[j, c], recv_sem=recv_sem.at[j, c],
            device_id=(partners[j], col), device_id_type=MESH,
        )

    half = leaf_v.shape[0]
    own_half = pl.ds(pl.multiple_of(col * half, half), half)
    leaf_here = pltpu.make_async_copy(leaf_v, lv.at[own_half], lv_sem)
    leaf_there = pltpu.make_async_remote_copy(
        src_ref=leaf_v, dst_ref=lv.at[own_half], send_sem=leaf_send, recv_sem=leaf_recv,
        device_id=(row, 1 - col), device_id_type=MESH,
    )
    mv_copies = [pltpu.make_async_copy(merge_v.at[j], mv.at[j], mv_sem.at[j]) for j in range(levels)]
    mt_copies = [pltpu.make_async_copy(merge_t.at[j], mt.at[j], mt_sem.at[j]) for j in range(levels)]
    lt_copy = pltpu.make_async_copy(leaf_t, lt, lt_sem)

    mv_copies[0].start()
    for c in range(LOOK):
        upper_copy(c).start()
    for j in range(levels):
        mt_copies[j].start()
        if j > 0:
            mv_copies[j].start()
    leaf_here.start()
    lt_copy.start()

    def load(c, carry):
        upper_copy(c).start()
        return carry

    def load_low(c, carry):
        lower_copy(c).start()
        return carry

    lax.fori_loop(LOOK, chunks, load, 0)
    lax.fori_loop(0, chunks, load_low, 0)

    barrier = pltpu.get_barrier_semaphore()
    for j in range(levels):
        pl.semaphore_signal(barrier, inc=1, device_id=(partners[j], col), device_id_type=MESH)
    pl.semaphore_signal(barrier, inc=1, device_id=(row, 1 - col), device_id_type=MESH)

    def prepare_v(j):
        mv_copies[j].wait()
        v = mv[j]
        vt2[j] = split_rows(v.T)
        v2[j] = split_rows(v)

    def prepare_t(j):
        mt_copies[j].wait()
        t2[j] = split_rows(mt[j])

    def first(c):
        upper_copy(c).wait()
        sent[0, c] = times(vt2.at[0], x[c, :width])
        exchange(0, c).start()

    prepare_v(0)
    pl.semaphore_wait(barrier, levels + 1)
    for c in range(LOOK):
        first(c)
    leaf_there.start()
    prepare_t(0)
    for j in range(1, levels):
        prepare_v(j)
        prepare_t(j)
    leaf_here.wait()
    lt_copy.wait()
    r2[...] = split_rows(lt[...])
    leaf_there.wait()
    whole = lv[...]
    l2[...] = split_rows(whole)
    lt2[...] = split_rows(whole.T)

    def merged(j, c):
        exchange(j, c).wait_recv()
        weights = times(t2.at[j], sent[j, c] + got[j, c])
        return x[c, :width] - times(v2.at[j], weights)

    def middle(j, c):
        upper = merged(j, c)
        x[c, :width] = upper
        sent[j + 1, c] = times(vt2.at[j + 1], upper)
        exchange(j + 1, c).start()

    def last(c):
        lower_copy(c).wait()
        x[c, :width] = merged(levels - 1, c)
        block = x[c]
        inner = times(r2, times(lt2, block))
        x[c] = block - times(l2, inner)
        out_copy(c).start()

    lags = [0] + [FIRST_LAG + j for j in range(levels - 1)]

    def step(t, carry):
        @pl.when(t + LOOK < chunks)
        def _():
            first(t + LOOK)

        for j in reversed(range(levels)):
            c = t - lags[j]

            @pl.when((c >= 0) & (c < chunks))
            def _():
                if j == levels - 1:
                    last(c)
                else:
                    middle(j, c)

        return carry

    lax.fori_loop(0, chunks + lags[-1], step, 0)

    def drain(c, carry):
        for j in range(levels):
            exchange(j, c).wait_send()
        out_copy(c).wait()
        return carry

    lax.fori_loop(0, chunks, drain, 0)


def body(rhs, leaf_v, leaf_t, merge_v, merge_t):
    rows, cols = rhs.shape
    levels, width = merge_v.shape[0], leaf_t.shape[1]
    chunks = cols // WIDTH
    f32, bf16 = jnp.float32, jnp.bfloat16
    dma = pltpu.SemaphoreType.DMA
    anywhere = pl.BlockSpec(memory_space=pl.ANY)
    return pl.pallas_call(
        kernel,
        out_shape=jax.ShapeDtypeStruct((rows, cols), f32),
        in_specs=[anywhere] * 5,
        out_specs=anywhere,
        scratch_shapes=[
            pltpu.VMEM((chunks, rows, WIDTH), f32),
            pltpu.VMEM((levels, chunks, width, WIDTH), f32),
            pltpu.VMEM((levels, chunks, width, WIDTH), f32),
            pltpu.VMEM((levels, width, width), f32),
            pltpu.VMEM((levels, width, width), f32),
            pltpu.VMEM((rows, width), f32),
            pltpu.VMEM((width, width), f32),
            pltpu.VMEM((levels, 2 * width, width), bf16),
            pltpu.VMEM((levels, 2 * width, width), bf16),
            pltpu.VMEM((levels, 2 * width, width), bf16),
            pltpu.VMEM((2 * rows, width), bf16),
            pltpu.VMEM((2 * width, rows), bf16),
            pltpu.VMEM((2 * width, width), bf16),
            dma((chunks,)),
            dma((chunks,)),
            dma((chunks,)),
            dma((levels,)),
            dma((levels,)),
            dma,
            dma,
            dma,
            dma,
            dma((levels, chunks)),
            dma((levels, chunks)),
        ],
        compiler_params=pltpu.CompilerParams(
            collective_id=0, has_side_effects=True, vmem_limit_bytes=48 * 1024 * 1024
        ),
    )(rhs, leaf_v, leaf_t, merge_v, merge_t)


def solution(mesh):
    return jax.shard_map(
        body,
        mesh=mesh,
        in_specs=(
            P("rows", "cols"),
            P(("rows", "cols"), None),
            P("rows", None),
            P(None, "rows", None),
            P(None, "rows", None),
        ),
        out_specs=P("rows", "cols"),
        check_vma=False,
    )
```

time: 295 us -> 150 us (0.51); the launches traced: 291 us -> 149 us
  waiting for transfers between devices: 223 us -> 0 us
  Pallas kernels: 0 us -> 140 us
  matrix products: 58.1 us -> 0 us
  local copies, waits for them, and re-layouts: 0.16 us -> 9.05 us
  starting transfers between devices: 7.55 us -> 0 us
    ppermute x4 -> x0, waiting for transfers between devices: 223 us -> none  [from_partner(): lax.ppermute(value, axis, [(i, i ^ 1 << apart) for i in range(lax.axis_si...]
    pallas_call x0 -> x1, Pallas kernels: none -> 140 us  [body(): pl.pallas_call(kernel, out_shape=jax.ShapeDtypeStruct((rows, cols), f32),...]
    dot_general x15 -> x0, matrix products: 58.1 us -> none  [the longest x4 25.9 us: body(): own_terms = jnp.einsum('nk,nj->kj', merge_block, upper_rows, precision=HIGH)]
    unnamed x10 -> x9, local copies, waits for them, and re-layouts: 0.03 us -> 9.05 us
    ppermute x4 -> x0, starting transfers between devices: 7.55 us -> none  [from_partner(): lax.ppermute(value, axis, [(i, i ^ 1 << apart) for i in range(lax.axis_si...]
  transfers between devices with their start and end apart: 4 -> 0, of which waited for: 4 -> 0; matrix products, arithmetic and copies ran while one was open for 0% -> 0% of each run, Pallas kernels for 0% -> 0%
where the time goes in v1:
time: 150 us; the launch traced here: 149 us
  Pallas kernels  140 us (93%)
  local copies, waits for them, and re-layouts  9.05 us (6%)
    pallas_call x1, Pallas kernels, body(): pl.pallas_call(kernel, out_shape=jax.ShapeDtypeStruct((rows, cols), f32),...  140 us
    unnamed x9, local copies, waits for them, and re-layouts  9.05 us

profile of v1, /device:TPU:0, one launch (start us, length us, event | category | flops | bytes accessed | tf_op | source)
XLA Modules:
  0.0 149.4 jit_solution(3359458750850332546)
XLA Ops:
  0.0 0.0 copy-start
  0.0 1.2 copy-done
  1.2 0.0 copy-start.1
  1.2 1.2 copy-done.1
  2.5 0.0 copy-start.2
  2.5 0.9 copy-done.2
  3.4 0.0 copy-start.3
  3.4 0.9 copy-done.3
  4.4 140.3 %shard_map.55 = f32[512,2048]{1,0:T(8,128)} custom-call(f32[512,2048]{1,0:T(8,128)} %rhs.1, f32[256,256]{1,0:T(8,128)S(1)} %copy-done.2, f32[256,256]{1,0:T(8,128)S(1)} %copy-done.3, f32[4,256,256]{2,1,0:T(8,128)S(1)} %copy-done, f32[4,256,256]{2,1,0:T(8,128)S(1)} %copy-done.1), custom_call_target="tpu_custom_call" | custom-call | tf_op jit(solution)/shard_map/pallas_call | solution.py:193
  144.7 4.7 %copy.7 = f32[512,2048]{1,0:T(8,128)} copy(f32[512,2048]{1,0:T(8,128)} %shard_map.55) | data formatting | bytes 8388608
Async XLA Ops:
  0.0 1.2 copy-start
  1.2 1.2 copy-start.1
  2.5 0.9 copy-start.2
  3.4 0.9 copy-start.3

commit v2 on v1

v2 whole, which is shorter than its diff:
```python
import functools

import jax
import jax.numpy as jnp
from jax import lax
from jax.experimental import pallas as pl
from jax.experimental.pallas import tpu as pltpu
from jax.sharding import PartitionSpec as P

MESH = pl.DeviceIdType.MESH
WIDTH = 256
OWN_LOOK = 4
FAR_LOOK = 2
LAG = 2


def halves(x):
    hi = x.astype(jnp.bfloat16)
    return hi, (x - hi.astype(jnp.float32)).astype(jnp.bfloat16)


def split(w):
    hi, lo = halves(w)
    return jnp.concatenate([hi, hi, lo], axis=1)


def times(w_ref, x):
    hi, lo = halves(x)
    return jnp.dot(w_ref[...], jnp.concatenate([hi, lo, hi], axis=0), preferred_element_type=jnp.float32)


def kernel(
    rhs, leaf_v, leaf_t, merge_v, merge_t, out,
    x, sent, got, mv, mt, lv, lt, far, v2, vt2, t2, far_v2, far_vt2, far_t2, l2, lt2, r2,
    up_sem, low_sem, out_sem, mv_sem, mt_sem, lv_sem, lt_sem, leaf_send, leaf_recv, far_send, far_recv, send_sem, recv_sem,
):
    levels, width = merge_v.shape[0], leaf_t.shape[1]
    chunks = x.shape[0]
    depth = lax.axis_size("rows").bit_length() - 1
    row, col = lax.axis_index("rows"), lax.axis_index("cols")
    partners, bits = [], []
    for j in range(levels):
        stride = 1 << (depth - 1 - j)
        bits.append((row // stride) % 2)
        partners.append(row + stride * (1 - 2 * bits[j]))
    beside = partners[1]
    across = partners[0] + partners[1] - row
    inner = bits[0] != bits[1]
    outer = bits[0] == bits[1]

    def columns(c):
        return pl.ds(pl.multiple_of(c * WIDTH, WIDTH), WIDTH)

    def upper_copy(c):
        return pltpu.make_async_copy(rhs.at[pl.ds(0, width), columns(c)], x.at[c, pl.ds(0, width)], up_sem.at[c])

    def lower_copy(c):
        low = pl.ds(width, x.shape[1] - width)
        return pltpu.make_async_copy(rhs.at[low, columns(c)], x.at[c, low], low_sem.at[c])

    def out_copy(c):
        return pltpu.make_async_copy(x.at[c], out.at[:, columns(c)], out_sem.at[c])

    def remote(src, slot, c, device):
        return pltpu.make_async_remote_copy(
            src_ref=src, dst_ref=got.at[slot, c],
            send_sem=send_sem.at[slot, c], recv_sem=recv_sem.at[slot, c],
            device_id=(device, col), device_id_type=MESH,
        )

    def cross(slot, c):
        return remote(sent.at[slot, c], slot, c, across)

    def hand_over(c):
        return remote(x.at[c, pl.ds(0, width)], 2, c, beside)

    def hand_back(c):
        return remote(sent.at[2, c], 2, c, beside)

    def exchange(j, c):
        return remote(sent.at[j + 1, c], j + 1, c, partners[j])

    half = leaf_v.shape[0]
    own_half = pl.ds(pl.multiple_of(col * half, half), half)
    leaf_here = pltpu.make_async_copy(leaf_v, lv.at[own_half], lv_sem)
    leaf_there = pltpu.make_async_remote_copy(
        src_ref=leaf_v, dst_ref=lv.at[own_half], send_sem=leaf_send, recv_sem=leaf_recv,
        device_id=(row, 1 - col), device_id_type=MESH,
    )
    mv_copies = [pltpu.make_async_copy(merge_v.at[j], mv.at[j], mv_sem.at[j]) for j in range(levels)]
    mt_copies = [pltpu.make_async_copy(merge_t.at[j], mt.at[j], mt_sem.at[j]) for j in range(levels)]
    lt_copy = pltpu.make_async_copy(leaf_t, lt, lt_sem)
    far_copies = [
        pltpu.make_async_remote_copy(
            src_ref=src, dst_ref=far.at[i], send_sem=far_send.at[i], recv_sem=far_recv.at[i],
            device_id=(beside, col), device_id_type=MESH,
        )
        for i, src in enumerate((merge_v.at[0], merge_t.at[0], merge_v.at[1]))
    ]

    mv_copies[0].start()
    barrier = pltpu.get_barrier_semaphore()
    for device in [across, beside] + partners[2:]:
        pl.semaphore_signal(barrier, inc=1, device_id=(device, col), device_id_type=MESH)
    pl.semaphore_signal(barrier, inc=1, device_id=(row, 1 - col), device_id_type=MESH)

    def load(c, carry):
        upper_copy(c).start()
        return carry

    def load_low(c, carry):
        lower_copy(c).start()
        return carry

    lax.fori_loop(0, chunks, load, 0)
    for j in range(levels):
        mt_copies[j].start()
        if j > 0:
            mv_copies[j].start()
    leaf_here.start()
    lt_copy.start()
    lax.fori_loop(0, chunks, load_low, 0)

    def prepare_v(j):
        mv_copies[j].wait()
        v = mv[j]
        vt2[j] = split(v.T)
        v2[j] = split(v)

    def prepare_t(j):
        mt_copies[j].wait()
        t2[j] = split(mt[j])

    def prepare_far(i):
        far_copies[i].wait_recv()
        if i == 1:
            far_t2[...] = split(far[1])
        else:
            v = far[i]
            far_vt2[i // 2] = split(v.T)
            far_v2[i // 2] = split(v)

    def first_own(c):
        upper_copy(c).wait()
        sent[0, c] = times(vt2.at[0], x[c, :width])
        cross(0, c).start()

    def first_far(c):
        hand_back(c).wait_recv()
        sent[1, c] = times(far_vt2.at[0], got[2, c])
        cross(1, c).start()

    prepare_v(0)
    pl.semaphore_wait(barrier, levels + 1)

    def give(c, carry):
        upper_copy(c).wait()
        hand_over(c).start()
        return carry

    @pl.when(outer)
    def _():
        far_copies[0].start()
        give(0, 0)
        give(1, 0)
        far_copies[1].start()
        far_copies[2].start()
        lax.fori_loop(2, chunks, give, 0)

    @pl.when(inner)
    def _():
        for c in range(OWN_LOOK):
            first_own(c)

    leaf_there.start()
    prepare_t(0)
    for j in range(1, levels):
        prepare_v(j)
        prepare_t(j)
    leaf_here.wait()
    lt_copy.wait()
    r2[...] = split(lt[...])

    @pl.when(inner)
    def _():
        prepare_far(0)
        for c in range(FAR_LOOK):
            first_far(c)
        prepare_far(1)
        prepare_far(2)

    leaf_there.wait()
    whole = lv[...]
    l2[...] = split(whole)
    lt2[...] = split(whole.T)

    def send_on(j, c, upper):
        x[c, :width] = upper
        sent[j + 1, c] = times(vt2.at[j], upper)
        exchange(j, c).start()

    def two_levels(c):
        cross(0, c).wait_recv()
        cross(1, c).wait_recv()
        far_w = times(far_t2, sent[1, c] + got[0, c])
        own_w = times(t2.at[0], sent[0, c] + got[1, c])
        far_u = got[2, c] - times(far_v2.at[0], far_w)
        own_u = x[c, :width] - times(v2.at[0], own_w)
        both = times(vt2.at[1], own_u) + times(far_vt2.at[1], far_u)
        pair_w = times(t2.at[1], both)
        sent[2, c] = far_u - times(far_v2.at[1], pair_w)
        hand_back(c).start()
        send_on(2, c, own_u - times(v2.at[1], pair_w))

    def take_back(c):
        hand_over(c).wait()
        send_on(2, c, got[2, c])

    def merged(j, c):
        exchange(j, c).wait_recv()
        weights = times(t2.at[j], sent[j + 1, c] + got[j + 1, c])
        return x[c, :width] - times(v2.at[j], weights)

    def last(c):
        lower_copy(c).wait()
        x[c, :width] = merged(levels - 1, c)
        block = x[c]
        inner_w = times(r2, times(lt2, block))
        x[c] = block - times(l2, inner_w)
        out_copy(c).start()

    def step(t, carry):
        @pl.when(inner & (t + OWN_LOOK < chunks))
        def _():
            first_own(t + OWN_LOOK)

        @pl.when(inner & (t + FAR_LOOK < chunks))
        def _():
            first_far(t + FAR_LOOK)

        for j in reversed(range(2, levels)):
            c = t - (j - 1) * LAG

            @pl.when((c >= 0) & (c < chunks))
            def _():
                if j == levels - 1:
                    last(c)
                else:
                    send_on(j + 1, c, merged(j, c))

        @pl.when(inner & (t < chunks))
        def _():
            two_levels(t)

        @pl.when(outer & (t < chunks))
        def _():
            take_back(t)

        return carry

    lax.fori_loop(0, chunks + (levels - 2) * LAG, step, 0)

    def drain(c, carry):
        for j in range(2, levels):
            exchange(j, c).wait_send()
        out_copy(c).wait()
        return carry

    def drain_inner(c, carry):
        cross(0, c).wait_send()
        cross(1, c).wait_send()
        hand_back(c).wait_send()
        return carry

    @pl.when(inner)
    def _():
        lax.fori_loop(0, chunks, drain_inner, 0)

    @pl.when(outer)
    def _():
        for copy in far_copies:
            copy.wait_send()

    lax.fori_loop(0, chunks, drain, 0)


def body(rhs, leaf_v, leaf_t, merge_v, merge_t):
    rows, cols = rhs.shape
    levels, width = merge_v.shape[0], leaf_t.shape[1]
    chunks = cols // WIDTH
    f32, bf16 = jnp.float32, jnp.bfloat16
    dma = pltpu.SemaphoreType.DMA
    anywhere = pl.BlockSpec(memory_space=pltpu.HBM)
    return pl.pallas_call(
        kernel,
        out_shape=jax.ShapeDtypeStruct((rows, cols), f32),
        in_specs=[anywhere] * 5,
        out_specs=anywhere,
        scratch_shapes=[
            pltpu.VMEM((chunks, rows, WIDTH), f32),
            pltpu.VMEM((levels + 1, chunks, width, WIDTH), f32),
            pltpu.VMEM((levels + 1, chunks, width, WIDTH), f32),
            pltpu.VMEM((levels, width, width), f32),
            pltpu.VMEM((levels, width, width), f32),
            pltpu.VMEM((rows, width), f32),
            pltpu.VMEM((width, width), f32),
            pltpu.VMEM((3, width, width), f32),
            pltpu.VMEM((levels, width, 3 * width), bf16),
            pltpu.VMEM((levels, width, 3 * width), bf16),
            pltpu.VMEM((levels, width, 3 * width), bf16),
            pltpu.VMEM((2, width, 3 * width), bf16),
            pltpu.VMEM((2, width, 3 * width), bf16),
            pltpu.VMEM((width, 3 * width), bf16),
            pltpu.VMEM((rows, 3 * width), bf16),
            pltpu.VMEM((width, 3 * rows), bf16),
            pltpu.VMEM((width, 3 * width), bf16),
            dma((chunks,)),
            dma((chunks,)),
            dma((chunks,)),
            dma((levels,)),
            dma((levels,)),
            dma,
            dma,
            dma,
            dma,
            dma((3,)),
            dma((3,)),
            dma((levels + 1, chunks)),
            dma((levels + 1, chunks)),
        ],
        compiler_params=pltpu.CompilerParams(
            collective_id=0, has_side_effects=True, vmem_limit_bytes=62 * 1024 * 1024
        ),
    )(rhs, leaf_v, leaf_t, merge_v, merge_t)


def solution(mesh):
    return jax.shard_map(
        body,
        mesh=mesh,
        in_specs=(
            P("rows", "cols"),
            P(("rows", "cols"), None),
            P("rows", None),
            P(None, "rows", None),
            P(None, "rows", None),
        ),
        out_specs=P("rows", "cols"),
        check_vma=False,
    )
```

time: 150 us -> 128 us (0.85)
  Pallas kernels: 140 us -> 123 us
  local copies, waits for them, and re-layouts: 9.05 us -> 4.7 us
    pallas_call x1, Pallas kernels: 140 us -> 123 us  [body(): pl.pallas_call(kernel, out_shape=jax.ShapeDtypeStruct((rows, cols), f32),...]
    unnamed x9 -> x1, local copies, waits for them, and re-layouts: 9.05 us -> 4.7 us
where the time goes in v2:
time: 128 us; the launch traced here: 127 us
  Pallas kernels  123 us (96%)
  local copies, waits for them, and re-layouts  4.7 us (4%)
    pallas_call x1, Pallas kernels, body(): pl.pallas_call(kernel, out_shape=jax.ShapeDtypeStruct((rows, cols), f32),...  123 us
    unnamed x1, local copies, waits for them, and re-layouts  4.7 us

profile of v2, /device:TPU:0, one launch (start us, length us, event | category | flops | bytes accessed | tf_op | source)
XLA Modules:
  0.0 127.4 jit_solution(4964646322972316778)
XLA Ops:
  0.0 122.7 %shard_map.55 = f32[512,2048]{1,0:T(8,128)} custom-call(f32[512,2048]{1,0:T(8,128)} %rhs.1, f32[256,256]{1,0:T(8,128)} %leaf_v.1, f32[256,256]{1,0:T(8,128)} %leaf_t.1, f32[4,256,256]{2,1,0:T(8,128)} %merge_v.1, f32[4,256,256]{2,1,0:T(8,128)} %merge_t.1), custom_call_target="tpu_custom_call" | custom-call | tf_op jit(solution)/shard_map/pallas_call | solution.py:294
  122.7 4.7 %copy.7 = f32[512,2048]{1,0:T(8,128)} copy(f32[512,2048]{1,0:T(8,128)} %shard_map.55) | data formatting | bytes 8388608

commit v3 on v2

--- a/solution.py
+++ b/solution.py
@@ -8,9 +8,10 @@
 from jax.sharding import PartitionSpec as P
 
 MESH = pl.DeviceIdType.MESH
-WIDTH = 256
+WIDTH = 128
+SINGLES = 4
 OWN_LOOK = 4
-FAR_LOOK = 2
+FAR_LOOK = 3
 LAG = 2
 
 
@@ -31,7 +32,7 @@
 
 def kernel(
     rhs, leaf_v, leaf_t, merge_v, merge_t, out,
-    x, sent, got, mv, mt, lv, lt, far, v2, vt2, t2, far_v2, far_vt2, far_t2, l2, lt2, r2,
+    x, sent, got, mv, mt, lv, lt, far, v2, vt2, far_v2, far_vt2, l2, lt2,
     up_sem, low_sem, out_sem, mv_sem, mt_sem, lv_sem, lt_sem, leaf_send, leaf_recv, far_send, far_recv, send_sem, recv_sem,
 ):
     levels, width = merge_v.shape[0], leaf_t.shape[1]
@@ -129,26 +130,61 @@
 
     def prepare_t(j):
         mt_copies[j].wait()
-        t2[j] = split(mt[j])
+        v2[j] = split(times(v2.at[j], mt[j]))
 
     def prepare_far(i):
         far_copies[i].wait_recv()
         if i == 1:
-            far_t2[...] = split(far[1])
+            far_v2[0] = split(times(far_v2.at[0], far[1]))
         else:
             v = far[i]
             far_vt2[i // 2] = split(v.T)
             far_v2[i // 2] = split(v)
-
-    def first_own(c):
-        upper_copy(c).wait()
-        sent[0, c] = times(vt2.at[0], x[c, :width])
-        cross(0, c).start()
-
-    def first_far(c):
-        hand_back(c).wait_recv()
-        sent[1, c] = times(far_vt2.at[0], got[2, c])
-        cross(1, c).start()
+            if i == 2:
+                far_v2[1] = split(times(far_v2.at[1], mt[1]))
+
+    singles = min(SINGLES, chunks)
+    pairs = (chunks - singles) // 2
+    units = pairs + chunks - 2 * pairs
+
+    def read(ref, c, n):
+        return jnp.concatenate([ref[c + i] for i in range(n)], axis=1)
+
+    def write(ref, c, n, value):
+        for i in range(n):
+            ref[c + i] = value[:, i * WIDTH : (i + 1) * WIDTH]
+
+    def read_upper(c, n):
+        return jnp.concatenate([x[c + i, :width] for i in range(n)], axis=1)
+
+    def write_upper(c, n, value):
+        for i in range(n):
+            x[c + i, :width] = value[:, i * WIDTH : (i + 1) * WIDTH]
+
+    def on_unit(stage, u, take):
+        take = take & (u >= 0) & (u < units)
+
+        @pl.when(take & (u < pairs))
+        def _():
+            stage(2 * u, 2)
+
+        @pl.when(take & (u >= pairs))
+        def _():
+            stage(pairs + u, 1)
+
+    def first_own(c, n):
+        for i in range(n):
+            upper_copy(c + i).wait()
+        write(sent.at[0], c, n, times(vt2.at[0], read_upper(c, n)))
+        for i in range(n):
+            cross(0, c + i).start()
+
+    def first_far(c, n):
+        for i in range(n):
+            hand_back(c + i).wait_recv()
+        write(sent.at[1], c, n, times(far_vt2.at[0], read(got.at[2], c, n)))
+        for i in range(n):
+            cross(1, c + i).start()
 
     prepare_v(0)
     pl.semaphore_wait(barrier, levels + 1)
@@ -164,13 +200,15 @@
         give(0, 0)
         give(1, 0)
         far_copies[1].start()
+        give(2, 0)
+        give(3, 0)
         far_copies[2].start()
-        lax.fori_loop(2, chunks, give, 0)
+        lax.fori_loop(4, chunks, give, 0)
 
     @pl.when(inner)
     def _():
-        for c in range(OWN_LOOK):
-            first_own(c)
+        for u in range(OWN_LOOK):
+            first_own(2 * u, 2)
 
     leaf_there.start()
     prepare_t(0)
@@ -179,86 +217,74 @@
         prepare_t(j)
     leaf_here.wait()
     lt_copy.wait()
-    r2[...] = split(lt[...])
 
     @pl.when(inner)
     def _():
         prepare_far(0)
-        for c in range(FAR_LOOK):
-            first_far(c)
+        for u in range(FAR_LOOK):
+            first_far(2 * u, 2)
         prepare_far(1)
         prepare_far(2)
 
     leaf_there.wait()
     whole = lv[...]
     l2[...] = split(whole)
+    l2[...] = split(times(l2, lt[...]))
     lt2[...] = split(whole.T)
 
-    def send_on(j, c, upper):
-        x[c, :width] = upper
-        sent[j + 1, c] = times(vt2.at[j], upper)
-        exchange(j, c).start()
-
-    def two_levels(c):
-        cross(0, c).wait_recv()
-        cross(1, c).wait_recv()
-        far_w = times(far_t2, sent[1, c] + got[0, c])
-        own_w = times(t2.at[0], sent[0, c] + got[1, c])
-        far_u = got[2, c] - times(far_v2.at[0], far_w)
-        own_u = x[c, :width] - times(v2.at[0], own_w)
+    def send_on(j, c, n, upper):
+        write_upper(c, n, upper)
+        write(sent.at[j + 1], c, n, times(vt2.at[j], upper))
+        for i in range(n):
+            exchange(j, c + i).start()
+
+    def two_levels(c, n):
+        for i in range(n):
+            cross(0, c + i).wait_recv()
+            cross(1, c + i).wait_recv()
+        far_sum = read(sent.at[1], c, n) + read(got.at[0], c, n)
+        own_sum = read(sent.at[0], c, n) + read(got.at[1], c, n)
+        far_u = read(got.at[2], c, n) - times(far_v2.at[0], far_sum)
+        own_u = read_upper(c, n) - times(v2.at[0], own_sum)
         both = times(vt2.at[1], own_u) + times(far_vt2.at[1], far_u)
-        pair_w = times(t2.at[1], both)
-        sent[2, c] = far_u - times(far_v2.at[1], pair_w)
-        hand_back(c).start()
-        send_on(2, c, own_u - times(v2.at[1], pair_w))
-
-    def take_back(c):
-        hand_over(c).wait()
-        send_on(2, c, got[2, c])
-
-    def merged(j, c):
-        exchange(j, c).wait_recv()
-        weights = times(t2.at[j], sent[j + 1, c] + got[j + 1, c])
-        return x[c, :width] - times(v2.at[j], weights)
-
-    def last(c):
-        lower_copy(c).wait()
-        x[c, :width] = merged(levels - 1, c)
-        block = x[c]
-        inner_w = times(r2, times(lt2, block))
-        x[c] = block - times(l2, inner_w)
-        out_copy(c).start()
+        write(sent.at[2], c, n, far_u - times(far_v2.at[1], both))
+        for i in range(n):
+            hand_back(c + i).start()
+        send_on(2, c, n, own_u - times(v2.at[1], both))
+
+    def take_back(c, n):
+        for i in range(n):
+            hand_over(c + i).wait()
+        send_on(2, c, n, read(got.at[2], c, n))
+
+    def merged(j, c, n):
+        for i in range(n):
+            exchange(j, c + i).wait_recv()
+        return read_upper(c, n) - times(v2.at[j], read(sent.at[j + 1], c, n) + read(got.at[j + 1], c, n))
+
+    def middle(j, c, n):
+        send_on(j + 1, c, n, merged(j, c, n))
+
+    def last(c, n):
+        for i in range(n):
+            lower_copy(c + i).wait()
+        write_upper(c, n, merged(levels - 1, c, n))
+        block = read(x, c, n)
+        write(x, c, n, block - times(l2, times(lt2, block)))
+        for i in range(n):
+            out_copy(c + i).start()
 
     def step(t, carry):
-        @pl.when(inner & (t + OWN_LOOK < chunks))
-        def _():
-            first_own(t + OWN_LOOK)
-
-        @pl.when(inner & (t + FAR_LOOK < chunks))
-        def _():
-            first_far(t + FAR_LOOK)
-
+        on_unit(first_own, t + OWN_LOOK, inner)
+        on_unit(first_far, t + FAR_LOOK, inner)
         for j in reversed(range(2, levels)):
-            c = t - (j - 1) * LAG
-
-            @pl.when((c >= 0) & (c < chunks))
-            def _():
-                if j == levels - 1:
-                    last(c)
-                else:
-                    send_on(j + 1, c, merged(j, c))
-
-        @pl.when(inner & (t < chunks))
-        def _():
-            two_levels(t)
-
-        @pl.when(outer & (t < chunks))
-        def _():
-            take_back(t)
-
-        return carry
-
-    lax.fori_loop(0, chunks + (levels - 2) * LAG, step, 0)
+            stage = last if j == levels - 1 else functools.partial(middle, j)
+            on_unit(stage, t - (j - 1) * LAG, True)
+        on_unit(two_levels, t, inner)
+        on_unit(take_back, t, outer)
+        return carry
+
+    lax.fori_loop(0, units + (levels - 2) * LAG, step, 0)
 
     def drain(c, carry):
         for j in range(2, levels):
@@ -307,13 +333,10 @@
             pltpu.VMEM((3, width, width), f32),
             pltpu.VMEM((levels, width, 3 * width), bf16),
             pltpu.VMEM((levels, width, 3 * width), bf16),
-            pltpu.VMEM((levels, width, 3 * width), bf16),
             pltpu.VMEM((2, width, 3 * width), bf16),
             pltpu.VMEM((2, width, 3 * width), bf16),
-            pltpu.VMEM((width, 3 * width), bf16),
             pltpu.VMEM((rows, 3 * width), bf16),
             pltpu.VMEM((width, 3 * rows), bf16),
-            pltpu.VMEM((width, 3 * width), bf16),
             dma((chunks,)),
             dma((chunks,)),
             dma((chunks,)),

time: 128 us -> 123 us (0.961)
  Pallas kernels: 123 us -> 118 us
    pallas_call x1, Pallas kernels: 123 us -> 118 us  [body(): pl.pallas_call(kernel, out_shape=jax.ShapeDtypeStruct((rows, cols), f32),...]
where the time goes in v3:
time: 123 us
  Pallas kernels  118 us (96%)
  local copies, waits for them, and re-layouts  4.7 us (4%)
    pallas_call x1, Pallas kernels, body(): pl.pallas_call(kernel, out_shape=jax.ShapeDtypeStruct((rows, cols), f32),...  118 us
    unnamed x1, local copies, waits for them, and re-layouts  4.7 us

profile of v3, /device:TPU:0, one launch (start us, length us, event | category | flops | bytes accessed | tf_op | source)
XLA Modules:
  0.0 123.0 jit_solution(11559289860285255532)
XLA Ops:
  0.0 118.3 %shard_map.55 = f32[512,2048]{1,0:T(8,128)} custom-call(f32[512,2048]{1,0:T(8,128)} %rhs.1, f32[256,256]{1,0:T(8,128)} %leaf_v.1, f32[256,256]{1,0:T(8,128)} %leaf_t.1, f32[4,256,256]{2,1,0:T(8,128)} %merge_v.1, f32[4,256,256]{2,1,0:T(8,128)} %merge_t.1), custom_call_target="tpu_custom_call" | custom-call | tf_op jit(solution)/shard_map/pallas_call | solution.py:320
  118.3 4.7 %copy.7 = f32[512,2048]{1,0:T(8,128)} copy(f32[512,2048]{1,0:T(8,128)} %shard_map.55) | data formatting | bytes 8388608
